TPU v7x, 768 devices: a whole 4x8x12 slice. The times are simulated.
768 devices in a mesh: pipe: 32 (over x, y), seq: 24 (over z, core).
Axes of the slice: x: 4, y: 8, z: 12, core: 2. Of those that a mesh axis runs over, the one named last changes fastest.
Arguments:
- layer_input: bfloat16 [32, 1536, 2, 1536], P('pipe', 'seq'), may hold values from -1.5 to 1.5
- grad_out: bfloat16 [32, 1536, 2, 1536], P('pipe', 'seq'), may hold values from -6 to 6
- queries: bfloat16 [32, 1536, 2, 768], P('pipe', 'seq'), may hold values from -8 to 8
- keys_saved: bfloat16 [32, 1536, 2, 768], P('pipe', 'seq'), may hold values from -8 to 8
- values_saved: bfloat16 [32, 1536, 2, 768], P('pipe', 'seq'), may hold values from -6 to 6
- out_weight: bfloat16 [32, 768, 1536], P('pipe'), may hold values from -0.15625 to 0.15625
- qkv_weight: bfloat16 [32, 1536, 2304], P('pipe'), may hold values from -0.125 to 0.125
- ln_gain: bfloat16 [32, 1536], P('pipe'), may hold values from 0.099609375 to 1.8984375
- lengths: int32 [32, 2], P('pipe'), may hold values from 193 to 1536
Outputs:
- passed: bfloat16 [32, 1536, 2, 1536], P('pipe', 'seq')
All inputs are finite; a program needn't handle non-finite values.
Results may differ from a plain program's by a relative error of at most 0.0063.
Values may be sent and summed in bfloat16 or wider, within the bound.
No kernel may reach another device: no remote copies, remote signals or barrier semaphores. Data moves between devices by JAX's collectives and lax.ppermute only.
A program may use at most 64 MiB of HBM per device.

v0:
```python
import jax
import jax.numpy as jnp
from jax import lax
from jax.sharding import PartitionSpec as P

HEADS_W = 12
HD = 64


def passed_along(block, axis, distance):
    devices = range(lax.axis_size(axis))
    route = [((i - distance) % len(devices), i) for i in devices]
    return lax.ppermute(block, axis, route)


def norm_backward(inputs, norm_gain, upstream):
    row_mean = jnp.mean(inputs, axis=-1, keepdims=True)
    centred = inputs - row_mean
    row_var = jnp.mean(centred * centred, axis=-1, keepdims=True)
    inv_std = lax.rsqrt(row_var + 1e-05)
    normed = centred * inv_std
    scaled = upstream * norm_gain
    return inv_std * (
        scaled
        - jnp.mean(scaled, axis=-1, keepdims=True)
        - normed * jnp.mean(scaled * normed, axis=-1, keepdims=True)
    )


def attend(query_heads, key_heads, value_heads, grad_heads, key_lengths):
    length = query_heads.shape[0]
    pair_count = query_heads.shape[1] // HD
    factor = HD ** (-0.5)
    query_split = query_heads.reshape(length, pair_count, HD)
    key_split = key_heads.reshape(length, pair_count, HD)
    value_split = value_heads.reshape(length, pair_count, HD)
    grad_split = grad_heads.reshape(length, pair_count, HD)
    block = 512
    usable = jnp.arange(length)[None, None, :] < key_lengths[:, None, None]

    def one_block(carried, block_index):
        key_acc, value_acc = carried
        query_block = lax.dynamic_slice_in_dim(query_split, block_index * block, block, 0)
        grad_block = lax.dynamic_slice_in_dim(grad_split, block_index * block, block, 0)
        scores = (
            jnp.einsum("qph,kph->pqk", query_block, key_split, preferred_element_type=jnp.float32)
            * factor
        )
        masked = jnp.where(usable, scores, -jnp.inf)
        row_peak = jnp.max(masked, axis=-1, keepdims=True)
        exp_terms = jnp.exp(masked - row_peak)
        prob_full = exp_terms / jnp.sum(exp_terms, axis=-1, keepdims=True)
        prob_low = prob_full.astype(jnp.bfloat16)
        value_acc = value_acc + jnp.einsum(
            "pqk,qph->kph", prob_low, grad_block, preferred_element_type=jnp.float32
        )
        grad_prob = jnp.einsum(
            "qph,kph->pqk", grad_block, value_split, preferred_element_type=jnp.float32
        )
        row_delta = jnp.sum(prob_full * grad_prob, axis=-1, keepdims=True)
        grad_score = (prob_full * (grad_prob - row_delta)).astype(jnp.bfloat16)
        grad_query = (
            jnp.einsum("pqk,kph->qph", grad_score, key_split, preferred_element_type=jnp.float32)
            * factor
        ).astype(jnp.bfloat16)
        key_acc = key_acc + jnp.einsum(
            "pqk,qph->kph", grad_score, query_block, preferred_element_type=jnp.float32
        )
        return ((key_acc, value_acc), grad_query)

    empty_acc = jnp.zeros((length, pair_count, HD), jnp.float32)
    (key_acc, value_acc), query_blocks = lax.scan(
        one_block, (empty_acc, empty_acc), jnp.arange(length // block)
    )
    grad_query = query_blocks.reshape(length, pair_count * HD)
    grad_key = (key_acc * factor).astype(jnp.bfloat16).reshape(length, pair_count * HD)
    grad_value = value_acc.astype(jnp.bfloat16).reshape(length, pair_count * HD)
    return (grad_query, grad_key, grad_value)


def per_device(
    layer_input,
    grad_out,
    queries,
    keys_saved,
    values_saved,
    out_weight,
    qkv_weight,
    ln_gain,
    lengths,
):
    frames = grad_out.shape[1]
    record_count = grad_out.shape[2]
    feature_count = grad_out.shape[3]
    inner_width = out_weight.shape[1]
    row_count = frames * record_count
    flat_grad = grad_out[0].reshape(row_count, feature_count)
    query_cols = queries[0].reshape(frames, record_count * inner_width)
    key_cols = keys_saved[0].reshape(frames, record_count * inner_width)
    value_cols = values_saved[0].reshape(frames, record_count * inner_width)
    product = lax.dot_general(
        flat_grad, out_weight[0], (((1,), (1,)), ((), ())), preferred_element_type=jnp.float32
    )
    grad_cols = product.astype(jnp.bfloat16).reshape(frames, record_count * inner_width)
    query_heads, key_heads, value_heads, grad_heads = (
        lax.all_to_all(query_cols, "seq", split_axis=1, concat_axis=0, tiled=True),
        lax.all_to_all(key_cols, "seq", split_axis=1, concat_axis=0, tiled=True),
        lax.all_to_all(value_cols, "seq", split_axis=1, concat_axis=0, tiled=True),
        lax.all_to_all(grad_cols, "seq", split_axis=1, concat_axis=0, tiled=True),
    )
    pair_count = query_heads.shape[1] // HD
    pair_ids = lax.axis_index("seq") * pair_count + jnp.arange(pair_count)
    record_ids = pair_ids // HEADS_W
    key_lengths = jnp.sum(
        jnp.where(record_ids[:, None] == jnp.arange(record_count)[None, :], lengths[0][None, :], 0),
        axis=1,
    )
    grad_query, grad_key, grad_value = attend(
        query_heads, key_heads, value_heads, grad_heads, key_lengths
    )
    back_query, back_key, back_value = (
        lax.all_to_all(grad_query, "seq", split_axis=0, concat_axis=1, tiled=True),
        lax.all_to_all(grad_key, "seq", split_axis=0, concat_axis=1, tiled=True),
        lax.all_to_all(grad_value, "seq", split_axis=0, concat_axis=1, tiled=True),
    )
    joined = jnp.concatenate(
        [
            back_query.reshape(row_count, inner_width),
            back_key.reshape(row_count, inner_width),
            back_value.reshape(row_count, inner_width),
        ],
        axis=1,
    )
    grad_normed = lax.dot_general(
        joined, qkv_weight[0], (((1,), (1,)), ((), ())), preferred_element_type=jnp.float32
    )
    inputs = layer_input[0].reshape(row_count, feature_count).astype(jnp.float32)
    branch = norm_backward(inputs, ln_gain[0].astype(jnp.float32)[None, :], grad_normed)
    total = (flat_grad.astype(jnp.float32) + branch).astype(jnp.bfloat16)
    passed = passed_along(total, "pipe", -1)
    return passed.reshape(1, frames, record_count, feature_count)


def solution(mesh):
    placed = (
        P("pipe", "seq", None, None),
        P("pipe", "seq", None, None),
        P("pipe", "seq", None, None),
        P("pipe", "seq", None, None),
        P("pipe", "seq", None, None),
        P("pipe", None, None),
        P("pipe", None, None),
        P("pipe", None),
        P("pipe", None),
    )
    return jax.shard_map(
        per_device,
        mesh=mesh,
        in_specs=placed,
        out_specs=P("pipe", "seq", None, None),
        check_vma=False,
    )
```

profile of v0, /device:TPU:62, one launch (start us, length us, event | category | flops | bytes accessed | tf_op | source)
XLA Modules:
  0.0 231.6 jit_solution(5627711092294958488)
XLA Ops:
  4.2 15.4 %all-to-all-start.2 = ((bf16[24,2,2048]{2,1,0:T(2,128)(2,1)}), bf16[24,2,2048]{2,1,0:T(2,128)(2,1)S(1)}, u32[]{:S(2)}, u32[]{:S(2)}) async-start(bf16[24,2,2048]{2,1,0:T(2,128)(2,1)} %reshape.219), calls=%async_computation.2 | async-start | bytes 393216 | tf_op jit(solution)/shard_map/all_to_all | solution.py:109
  21.8 12.4 %all-to-all-done.2 = bf16[24,2,2048]{2,1,0:T(2,128)(2,1)S(1)} async-done(((bf16[24,2,2048]{2,1,0:T(2,128)(2,1)}), bf16[24,2,2048]{2,1,0:T(2,128)(2,1)S(1)}, u32[]{:S(2)}, u32[]{:S(2)}) %all-to-all-start.2) | async-done | bytes 196640 | tf_op jit(solution)/shard_map/all_to_all | solution.py:109
  34.9 3.8 %all-to-all-start = ((bf16[24,2,2048]{2,1,0:T(2,128)(2,1)}), bf16[24,2,2048]{2,1,0:T(2,128)(2,1)S(1)}, u32[]{:S(2)}, u32[]{:S(2)}) async-start(bf16[24,2,2048]{2,1,0:T(2,128)(2,1)} %reshape.215), calls=%async_computation | async-start | bytes 393216 | tf_op jit(solution)/shard_map/all_to_all | solution.py:106
  40.9 12.5 %all-to-all-done = bf16[24,2,2048]{2,1,0:T(2,128)(2,1)S(1)} async-done(((bf16[24,2,2048]{2,1,0:T(2,128)(2,1)}), bf16[24,2,2048]{2,1,0:T(2,128)(2,1)S(1)}, u32[]{:S(2)}, u32[]{:S(2)}) %all-to-all-start) | async-done | bytes 196640 | tf_op jit(solution)/shard_map/all_to_all | solution.py:106
  53.4 4.5 %all-to-all-start.1 = ((bf16[24,2,2048]{2,1,0:T(2,128)(2,1)}), bf16[24,2,2048]{2,1,0:T(2,128)(2,1)}, u32[]{:S(2)}, u32[]{:S(2)}) async-start(bf16[24,2,2048]{2,1,0:T(2,128)(2,1)} %reshape.217), calls=%async_computation.1 | async-start | bytes 393216 | tf_op jit(solution)/shard_map/all_to_all | solution.py:107
  62.0 10.6 %all-to-all-done.1 = bf16[24,2,2048]{2,1,0:T(2,128)(2,1)} async-done(((bf16[24,2,2048]{2,1,0:T(2,128)(2,1)}), bf16[24,2,2048]{2,1,0:T(2,128)(2,1)}, u32[]{:S(2)}, u32[]{:S(2)}) %all-to-all-start.1) | async-done | bytes 196640 | tf_op jit(solution)/shard_map/all_to_all | solution.py:107
  72.6 4.7 %all-to-all-start.3 = ((bf16[24,2,2048]{2,1,0:T(2,128)(2,1)}), bf16[24,2,2048]{2,1,0:T(2,128)(2,1)}, u32[]{:S(2)}, u32[]{:S(2)}) async-start(bf16[24,2,2048]{2,1,0:T(2,128)(2,1)} %reshape.221), calls=%async_computation.3 | async-start | bytes 393216 | tf_op jit(solution)/shard_map/all_to_all | solution.py:108
  82.1 2.0 reshape.218
  87.3 4.4 %all-to-all-done.3 = bf16[24,2,2048]{2,1,0:T(2,128)(2,1)} async-done(((bf16[24,2,2048]{2,1,0:T(2,128)(2,1)}), bf16[24,2,2048]{2,1,0:T(2,128)(2,1)}, u32[]{:S(2)}, u32[]{:S(2)}) %all-to-all-start.3) | async-done | bytes 196640 | tf_op jit(solution)/shard_map/all_to_all | solution.py:108
  91.7 2.0 reshape.222
  97.7 38.2 %while.15 = (s32[]{:T(128)}, f32[1536,1,64]{0,2,1:T(8,128)S(1)}, f32[1536,1,64]{0,2,1:T(8,128)}, bf16[3,512,1,64]{1,3,2,0:T(8,128)(2,1)}, s32[3]{0:T(128)S(1)}, ...) while((s32[]{:T(128)}, f32[1536,1,64]{0,2,1:T(8,128)S(1)}, ...), condition=%wide.region_7.8_spmd.clone, body=%wide.region_3.7_spmd.clone.sunk | while | flops 517144576 | bytes 55208240 | solution.py:72
  102.5 3.6 %fusion.70 = f32[1536,1,64]{0,2,1:T(8,128)} fusion(f32[1536,1,64]{0,2,1:T(8,128)} %get-tuple-element.212, pred[]{:T(512)S(6)} %compare.3, bf16[1536,1,64]{0,2,1:T(8,128)(2,1)} %get-tuple-element.231, s32[]{:T(128)S(6)} %select_n.27, f32[512,1536]{1,0:T(8,128)} %copy-done.1, f32[512]{0:T(512)S(1)} %fusion.68, f32[512]{0:T(512)S(1)} %get-tuple-element.193), kind=kOutput, calls=%fused_computation.9.clone.1 | convolution fusion | flops 103219200 | bytes 4001797 | tf_op jit(solution)/shard_map/while/body/eval_jaxpr/pqk,qph->kph/dot_general | solution.py:54
  115.2 3.6 %fusion.70 = f32[1536,1,64]{0,2,1:T(8,128)} fusion(f32[1536,1,64]{0,2,1:T(8,128)} %get-tuple-element.212, pred[]{:T(512)S(6)} %compare.3, bf16[1536,1,64]{0,2,1:T(8,128)(2,1)} %get-tuple-element.231, s32[]{:T(128)S(6)} %select_n.27, f32[512,1536]{1,0:T(8,128)} %copy-done.1, f32[512]{0:T(512)S(1)} %fusion.68, f32[512]{0:T(512)S(1)} %get-tuple-element.193), kind=kOutput, calls=%fused_computation.9.clone.1 | convolution fusion | flops 103219200 | bytes 4001797 | tf_op jit(solution)/shard_map/while/body/eval_jaxpr/pqk,qph->kph/dot_general | solution.py:54
  127.9 3.6 %fusion.70 = f32[1536,1,64]{0,2,1:T(8,128)} fusion(f32[1536,1,64]{0,2,1:T(8,128)} %get-tuple-element.212, pred[]{:T(512)S(6)} %compare.3, bf16[1536,1,64]{0,2,1:T(8,128)(2,1)} %get-tuple-element.231, s32[]{:T(128)S(6)} %select_n.27, f32[512,1536]{1,0:T(8,128)} %copy-done.1, f32[512]{0:T(512)S(1)} %fusion.68, f32[512]{0:T(512)S(1)} %get-tuple-element.193), kind=kOutput, calls=%fused_computation.9.clone.1 | convolution fusion | flops 103219200 | bytes 4001797 | tf_op jit(solution)/shard_map/while/body/eval_jaxpr/pqk,qph->kph/dot_general | solution.py:54
  137.7 2.0 all_to_all.96
  141.5 2.0 reshape.227
  143.5 5.1 %all-to-all-start.4 = ((bf16[24,2,2048]{2,1,0:T(2,128)(2,1)}), bf16[24,2,2048]{2,1,0:T(2,128)(2,1)}, u32[]{:S(2)}, u32[]{:S(2)}) async-start(bf16[24,2,2048]{2,1,0:T(2,128)(2,1)} %reshape.227), calls=%async_computation.4 | async-start | bytes 393216 | tf_op jit(solution)/shard_map/all_to_all | solution.py:122
  152.6 10.7 %all-to-all-done.4 = bf16[24,2,2048]{2,1,0:T(2,128)(2,1)} async-done(((bf16[24,2,2048]{2,1,0:T(2,128)(2,1)}), bf16[24,2,2048]{2,1,0:T(2,128)(2,1)}, u32[]{:S(2)}, u32[]{:S(2)}) %all-to-all-start.4) | async-done | bytes 196640 | tf_op jit(solution)/shard_map/all_to_all | solution.py:122
  163.2 4.5 %all-to-all-start.5 = ((bf16[24,2,2048]{2,1,0:T(2,128)(2,1)}), bf16[24,2,2048]{2,1,0:T(2,128)(2,1)}, u32[]{:S(2)}, u32[]{:S(2)}) async-start(bf16[24,2,2048]{2,1,0:T(2,128)(2,1)} %reshape.225), calls=%async_computation.5 | async-start | bytes 393216 | tf_op jit(solution)/shard_map/all_to_all | solution.py:123
  172.4 10.1 %all-to-all-done.5 = bf16[24,2,2048]{2,1,0:T(2,128)(2,1)} async-done(((bf16[24,2,2048]{2,1,0:T(2,128)(2,1)}), bf16[24,2,2048]{2,1,0:T(2,128)(2,1)}, u32[]{:S(2)}, u32[]{:S(2)}) %all-to-all-start.5) | async-done | bytes 196640 | tf_op jit(solution)/shard_map/all_to_all | solution.py:123
  182.4 4.7 %all-to-all-start.6 = ((bf16[24,2,2048]{2,1,0:T(2,128)(2,1)}), bf16[24,2,2048]{2,1,0:T(2,128)(2,1)}, u32[]{:S(2)}, u32[]{:S(2)}) async-start(bf16[24,2,2048]{2,1,0:T(2,128)(2,1)} %reshape.223), calls=%async_computation.6 | async-start | bytes 393216 | tf_op jit(solution)/shard_map/all_to_all | solution.py:124
  188.7 2.0 reshape.228
  194.4 2.0 reshape.203
  196.4 2.0 reshape.226
  198.4 2.0 copy.34
  200.4 2.0 reshape.204
  202.4 2.0 reshape.224
  204.3 2.0 copy.36
  206.3 2.0 reshape.205
  208.3 5.8 %fusion.45 = (f32[128]{0:T(128)S(1)}, f32[128]{0:T(128)S(1)}, f32[128,1536]{1,0:T(8,128)S(1)}) fusion(f32[128]{0:T(128)S(1)} %copy-done.10, f32[128,1536]{1,0:T(8,128)S(1)} %copy-done.3, f32[128]{0:T(128)S(1)} %copy-done.9, f32[1536]{0:T(1024)S(1)} %convert_reduce_fusion.1, bf16[1,1536,2304]{2,1,0:T(8,128)(2,1)} %param.17, bf16[128,768]{1,0:T(8,128)(2,1)} %reshape.205, ...), kind=kOutput, calls=%fused_computation.59 | convolution fusion | flops 908918528 | bytes 9248768 | tf_op jit(solution)/shard_map/dot_general | solution.py:134
  214.6 3.3 %collective-permute-start = (bf16[128,1536]{1,0:T(8,128)(2,1)S(1)}, bf16[128,1536]{1,0:T(8,128)(2,1)S(1)}, u32[]{:S(2)}, u32[]{:S(2)}) collective-permute-start(bf16[128,1536]{1,0:T(8,128)(2,1)S(1)} %add_convert_fusion), channel_id=1, source_target_pairs={{24,0},{48,24},{72,48},{96,72},{120,96},{144,120},{168,144},{192,1... | collective-permute-start | bytes 1179656 | tf_op jit(solution)/shard_map/ppermute | solution.py:13
  217.8 12.9 %collective-permute-done = bf16[128,1536]{1,0:T(8,128)(2,1)S(1)} collective-permute-done((bf16[128,1536]{1,0:T(8,128)(2,1)S(1)}, bf16[128,1536]{1,0:T(8,128)(2,1)S(1)}, u32[]{:S(2)}, u32[]{:S(2)}) %collective-permute-start) | collective-permute-done | bytes 393248 | tf_op jit(solution)/shard_map/ppermute | solution.py:13
  (112 shorter events, 69.4 us)
Async XLA Ops:
  0.0 1.8 copy-start
  2.9 57.3 %copy-start.11 = (s32[1,2]{1,0:T(1,128)S(1)}, s32[1,2]{1,0:T(1,128)}, u32[]{:S(2)}) copy-start(s32[1,2]{1,0:T(1,128)} %param.19) | copy-start | bytes 28
  4.2 29.9 %all-to-all-start.2 = ((bf16[24,2,2048]{2,1,0:T(2,128)(2,1)}), bf16[24,2,2048]{2,1,0:T(2,128)(2,1)S(1)}, u32[]{:S(2)}, u32[]{:S(2)}) async-start(bf16[24,2,2048]{2,1,0:T(2,128)(2,1)} %reshape.219), calls=%async_computation.2 | async-start | bytes 393216 | tf_op jit(solution)/shard_map/all_to_all | solution.py:109
  34.2 0.7 copy-start.6
  34.9 18.5 %all-to-all-start = ((bf16[24,2,2048]{2,1,0:T(2,128)(2,1)}), bf16[24,2,2048]{2,1,0:T(2,128)(2,1)S(1)}, u32[]{:S(2)}, u32[]{:S(2)}) async-start(bf16[24,2,2048]{2,1,0:T(2,128)(2,1)} %reshape.215), calls=%async_computation | async-start | bytes 393216 | tf_op jit(solution)/shard_map/all_to_all | solution.py:106
  53.4 4.6 %copy-start.5 = (bf16[24,2,2048]{2,1,0:T(2,128)(2,1)}, bf16[24,2,2048]{2,1,0:T(2,128)(2,1)S(1)}, u32[]{:S(2)}) copy-start(bf16[24,2,2048]{2,1,0:T(2,128)(2,1)S(1)} %all-to-all-done) | copy-start | bytes 589828
  53.4 19.2 %all-to-all-start.1 = ((bf16[24,2,2048]{2,1,0:T(2,128)(2,1)}), bf16[24,2,2048]{2,1,0:T(2,128)(2,1)}, u32[]{:S(2)}, u32[]{:S(2)}) async-start(bf16[24,2,2048]{2,1,0:T(2,128)(2,1)} %reshape.217), calls=%async_computation.1 | async-start | bytes 393216 | tf_op jit(solution)/shard_map/all_to_all | solution.py:107
  72.6 19.1 %all-to-all-start.3 = ((bf16[24,2,2048]{2,1,0:T(2,128)(2,1)}), bf16[24,2,2048]{2,1,0:T(2,128)(2,1)}, u32[]{:S(2)}, u32[]{:S(2)}) async-start(bf16[24,2,2048]{2,1,0:T(2,128)(2,1)} %reshape.221), calls=%async_computation.3 | async-start | bytes 393216 | tf_op jit(solution)/shard_map/all_to_all | solution.py:108
  100.3 1.7 copy-start.1
  102.5 3.6 %copy-start.2 = (f32[512,1536]{1,0:T(8,128)S(1)}, f32[512,1536]{1,0:T(8,128)}, u32[]{:S(2)}) copy-start(f32[512,1536]{1,0:T(8,128)} %copy-done.1) | copy-start | bytes 9437188 | tf_op jit(solution)/shard_map/while
  102.5 3.6 %copy-start.7 = (bf16[1536,1,64]{0,2,1:T(8,128)(2,1)S(1)}, bf16[1536,1,64]{0,2,1:T(8,128)(2,1)}, u32[]{:S(2)}) copy-start(bf16[1536,1,64]{0,2,1:T(8,128)(2,1)} %get-tuple-element.232) | copy-start | bytes 589828 | tf_op jit(solution)/shard_map/while
  112.9 1.7 copy-start.1
  115.2 3.6 %copy-start.2 = (f32[512,1536]{1,0:T(8,128)S(1)}, f32[512,1536]{1,0:T(8,128)}, u32[]{:S(2)}) copy-start(f32[512,1536]{1,0:T(8,128)} %copy-done.1) | copy-start | bytes 9437188 | tf_op jit(solution)/shard_map/while
  115.2 3.6 %copy-start.7 = (bf16[1536,1,64]{0,2,1:T(8,128)(2,1)S(1)}, bf16[1536,1,64]{0,2,1:T(8,128)(2,1)}, u32[]{:S(2)}) copy-start(bf16[1536,1,64]{0,2,1:T(8,128)(2,1)} %get-tuple-element.232) | copy-start | bytes 589828 | tf_op jit(solution)/shard_map/while
  125.7 1.7 copy-start.1
  127.9 3.6 %copy-start.2 = (f32[512,1536]{1,0:T(8,128)S(1)}, f32[512,1536]{1,0:T(8,128)}, u32[]{:S(2)}) copy-start(f32[512,1536]{1,0:T(8,128)} %copy-done.1) | copy-start | bytes 9437188 | tf_op jit(solution)/shard_map/while
  127.9 3.6 %copy-start.7 = (bf16[1536,1,64]{0,2,1:T(8,128)(2,1)S(1)}, bf16[1536,1,64]{0,2,1:T(8,128)(2,1)}, u32[]{:S(2)}) copy-start(bf16[1536,1,64]{0,2,1:T(8,128)(2,1)} %get-tuple-element.232) | copy-start | bytes 589828 | tf_op jit(solution)/shard_map/while
  135.8 12.8 %copy-start.4 = (bf16[1,64,2,1536]{3,2,1,0:T(2,128)(2,1)S(1)}, bf16[1,64,2,1536]{3,2,1,0:T(2,128)(2,1)}, u32[]{:S(2)}) copy-start(bf16[1,64,2,1536]{3,2,1,0:T(2,128)(2,1)} %param.11) | copy-start | bytes 1179652
  143.5 19.7 %all-to-all-start.4 = ((bf16[24,2,2048]{2,1,0:T(2,128)(2,1)}), bf16[24,2,2048]{2,1,0:T(2,128)(2,1)}, u32[]{:S(2)}, u32[]{:S(2)}) async-start(bf16[24,2,2048]{2,1,0:T(2,128)(2,1)} %reshape.227), calls=%async_computation.4 | async-start | bytes 393216 | tf_op jit(solution)/shard_map/all_to_all | solution.py:122
  148.7 40.0 %copy-start.8 = (bf16[1,1536]{1,0:T(2,128)(2,1)S(1)}, bf16[1,1536]{1,0:T(2,128)(2,1)}, u32[]{:S(2)}) copy-start(bf16[1,1536]{1,0:T(2,128)(2,1)} %param.18) | copy-start | bytes 9220
  163.2 19.2 %all-to-all-start.5 = ((bf16[24,2,2048]{2,1,0:T(2,128)(2,1)}), bf16[24,2,2048]{2,1,0:T(2,128)(2,1)}, u32[]{:S(2)}, u32[]{:S(2)}) async-start(bf16[24,2,2048]{2,1,0:T(2,128)(2,1)} %reshape.225), calls=%async_computation.5 | async-start | bytes 393216 | tf_op jit(solution)/shard_map/all_to_all | solution.py:123
  182.4 20.0 %all-to-all-start.6 = ((bf16[24,2,2048]{2,1,0:T(2,128)(2,1)}), bf16[24,2,2048]{2,1,0:T(2,128)(2,1)}, u32[]{:S(2)}, u32[]{:S(2)}) async-start(bf16[24,2,2048]{2,1,0:T(2,128)(2,1)} %reshape.223), calls=%async_computation.6 | async-start | bytes 393216 | tf_op jit(solution)/shard_map/all_to_all | solution.py:124
  190.7 17.7 %copy-start.3 = (f32[128,1536]{1,0:T(8,128)S(1)}, f32[128,1536]{1,0:T(8,128)}, u32[]{:S(2)}) copy-start(f32[128,1536]{1,0:T(8,128)} %reshape.208) | copy-start | bytes 2359300
  190.7 17.7 %copy-start.9 = (f32[128]{0:T(128)S(1)}, f32[128]{0:T(128)}, u32[]{:S(2)}) copy-start(f32[128]{0:T(128)} %div.37) | copy-start | bytes 1540
  190.7 17.7 %copy-start.10 = (f32[128]{0:T(128)S(1)}, f32[128]{0:T(128)}, u32[]{:S(2)}) copy-start(f32[128]{0:T(128)} %rsqrt.12) | copy-start | bytes 1540
  214.6 16.2 %collective-permute-start = (bf16[128,1536]{1,0:T(8,128)(2,1)S(1)}, bf16[128,1536]{1,0:T(8,128)(2,1)S(1)}, u32[]{:S(2)}, u32[]{:S(2)}) collective-permute-start(bf16[128,1536]{1,0:T(8,128)(2,1)S(1)} %add_convert_fusion), channel_id=1, source_target_pairs={{24,0},{48,24},{72,48},{96,72},{120,96},{144,120},{168,144},{192,1... | collective-permute-start | bytes 1179656 | tf_op jit(solution)/shard_map/ppermute | solution.py:13
where the time goes:
time: 234 us; the launch traced here: 232 us
  waiting for transfers between devices  73.4 us (31%)
  local copies, waits for them, and re-layouts  68.7 us (29%)
  starting transfers between devices  46.1 us (20%)
  matrix products  30 us (13%)
  other arithmetic  11.1 us (5%)
    unnamed x35, local copies, waits for them, and re-layouts  25 us
    all_to_all x1, starting transfers between devices, per_device(): lax.all_to_all(grad_cols, 'seq', split_axis=1, concat_axis=0, tiled=True)  15.4 us
    ppermute x1, waiting for transfers between devices, passed_along(): return lax.ppermute(block, axis, route)  12.9 us
    all_to_all x1, waiting for transfers between devices, per_device(): lax.all_to_all(query_cols, 'seq', split_axis=1, concat_axis=0, tiled=True)  12.5 us
    all_to_all x1, waiting for transfers between devices, per_device(): lax.all_to_all(grad_cols, 'seq', split_axis=1, concat_axis=0, tiled=True)  12.4 us
    dot_general x3, matrix products, one_block(): jnp.einsum('pqk,qph->kph', prob_low, grad_block, preferred_element_type=j...  10.8 us
    all_to_all x1, waiting for transfers between devices, per_device(): lax.all_to_all(grad_query, 'seq', split_axis=0, concat_axis=1, tiled=True)  10.7 us
    all_to_all x1, waiting for transfers between devices, per_device(): lax.all_to_all(key_cols, 'seq', split_axis=1, concat_axis=0, tiled=True)  10.6 us
  transfers between devices with their start and end apart: 8, of which 7 were waited for; matrix products, arithmetic and copies ran while one was open for 18% of the time, Pallas kernels for 0%

commit v1 on v0

v1 whole, which is shorter than its diff:
```python
import jax
import jax.numpy as jnp
from jax import lax
from jax.experimental import pallas as pl
from jax.experimental.pallas import tpu as pltpu
from jax.sharding import PartitionSpec as P

HEADS_W = 12
HD = 64
LANES = 128
MASKED = -1e30
LOG2E = 1.4426950408889634
F32 = jnp.float32
BF16 = jnp.bfloat16
NT = (((1,), (1,)), ((), ()))


def passed_along(block, axis, distance):
    devices = range(lax.axis_size(axis))
    route = [((i - distance) % len(devices), i) for i in devices]
    return lax.ppermute(block, axis, route)


def low_half(shape):
    return lax.broadcasted_iota(jnp.int32, shape, len(shape) - 1) < HD


def one_hot_rows(rows, frames, records, to_interleaved):
    row = lax.broadcasted_iota(jnp.int32, (rows, rows), 0)
    col = lax.broadcasted_iota(jnp.int32, (rows, rows), 1)
    if to_interleaved:
        row, col = col, row
    hit = col == (row % frames) * records + row // frames
    return hit.astype(F32).astype(BF16)


def head_pair(left, right, low):
    turned = pltpu.roll(jnp.where(low, right, left), HD, 1)
    return jnp.where(low, left, turned), jnp.where(low, turned, right)


def pack_kernel(grad_ref, query_ref, key_ref, value_ref, weight_ref, sent_ref):
    frames, records, features = grad_ref.shape
    inner = weight_ref.shape[0]
    rows = frames * records
    order = one_hot_rows(rows, frames, records, False)

    def by_record(matrix):
        return jnp.dot(order, matrix, preferred_element_type=F32)

    flat_grad = grad_ref[...].reshape(rows, features)
    heads_grad = lax.dot_general(
        flat_grad, weight_ref[...], NT, preferred_element_type=F32
    ).astype(BF16)
    grad = by_record(heads_grad)
    query = by_record(query_ref[...].reshape(rows, inner))
    key = by_record(key_ref[...].reshape(rows, inner))
    value = by_record(value_ref[...].reshape(rows, inner))
    low = low_half((frames, LANES))
    for record in range(records):
        rs = slice(record * frames, (record + 1) * frames)
        for tile in range(inner // LANES):
            cs = slice(tile * LANES, (tile + 1) * LANES)
            pair = record * HEADS_W + 2 * tile
            qg = head_pair(query[rs, cs], grad[rs, cs], low)
            kv = head_pair(key[rs, cs], value[rs, cs], low)
            for side in range(2):
                sent_ref[pair + side, :, 0:LANES] = qg[side].astype(BF16)
                sent_ref[pair + side, :, LANES:] = kv[side].astype(BF16)


def attend_kernel(
    length_ref, heads_ref, back_ref, kt_ref, q_ref, g_ref, bias_ref, score_ref, prob_ref, acc_ref
):
    length = heads_ref.shape[0]
    devices, packed, _ = back_ref.shape
    frames = length // devices
    block = 256
    chunks = length // block
    record = lax.axis_index("seq") // HEADS_W
    key_length = jnp.where(record == 0, length_ref[0, 0], length_ref[0, 1])
    factor = HD ** (-0.5)
    rate = factor * LOG2E

    low = low_half((length, LANES))
    both = heads_ref[:, 0:LANES].astype(F32)
    q_ref[...] = jnp.where(low, both, 0.0).astype(BF16)
    g_ref[...] = jnp.where(low, 0.0, both).astype(BF16)
    kt_ref[...] = heads_ref[:, LANES:].astype(F32).T[0:HD].astype(BF16)
    bias_ref[...] = jnp.where(
        lax.broadcasted_iota(jnp.int32, (length, LANES), 0) < key_length, 0.0, MASKED
    )

    def fold(values, op):
        return op(values.reshape(-1, 8, block), axis=0)

    for qb in range(chunks):
        qs = slice(qb * block, (qb + 1) * block)
        q_blk = q_ref[qs, :]
        g_blk = g_ref[qs, :]
        peak = None
        for c in range(chunks):
            ks = slice(c * block, (c + 1) * block)
            bias = bias_ref[ks, :]
            scores = lax.dot_general(
                heads_ref[ks, LANES:], q_blk, NT, preferred_element_type=F32
            ) + jnp.concatenate([bias] * (block // LANES), axis=1)
            score_ref[ks, :] = scores
            part = fold(scores, jnp.max)
            peak = part if peak is None else jnp.maximum(peak, part)
        peak = jnp.max(peak, axis=0, keepdims=True)
        total = None
        weighted = None
        for c in range(chunks):
            ks = slice(c * block, (c + 1) * block)
            terms = jnp.exp2((score_ref[ks, :] - peak) * rate)
            grad_prob = lax.dot_general(
                heads_ref[ks, LANES:], g_blk, NT, preferred_element_type=F32
            )
            score_ref[ks, :] = terms
            prob_ref[ks, :] = grad_prob
            part = fold(terms, jnp.sum)
            total = part if total is None else total + part
            part = fold(terms * grad_prob, jnp.sum)
            weighted = part if weighted is None else weighted + part
        share = 1.0 / jnp.sum(total, axis=0, keepdims=True)
        delta = jnp.sum(weighted, axis=0, keepdims=True) * share
        grad_q = None
        for c in range(chunks):
            ks = slice(c * block, (c + 1) * block)
            prob = score_ref[ks, :] * share
            grad_score = (prob * (prob_ref[ks, :] - delta)).astype(BF16)
            update = jnp.dot(prob.astype(BF16), g_blk, preferred_element_type=F32) + jnp.dot(
                grad_score, q_blk, preferred_element_type=F32
            )
            if qb == 0:
                acc_ref[ks, :] = update
            else:
                acc_ref[ks, :] += update
            part = jnp.dot(kt_ref[:, ks], grad_score, preferred_element_type=F32)
            grad_q = part if grad_q is None else grad_q + part
        rows = (grad_q.T * factor).reshape(block // frames, frames, HD)
        half = frames // 2
        for j in range(block // frames):
            back_ref[qb * (block // frames) + j, frames:packed, :] = jnp.concatenate(
                [rows[j, 0:half], rows[j, half:]], axis=1
            ).astype(BF16)
    scale = jnp.where(low_half((1, LANES)), factor, 1.0)
    back_ref[:, 0:frames, :] = (acc_ref[...] * scale).astype(BF16).reshape(devices, frames, LANES)


def finish_kernel(back_ref, weight_ref, input_ref, grad_ref, gain_ref, out_ref, joined_ref):
    frames, records, features = grad_ref.shape
    rows = frames * records
    inner = weight_ref.shape[1] // 3
    half = frames // 2
    low = low_half((frames, LANES))
    low_part = low_half((half, LANES))
    for record in range(records):
        base = record * frames
        for tile in range(inner // LANES):
            pair = record * HEADS_W + 2 * tile
            first = back_ref[pair].astype(F32)
            second = back_ref[pair + 1].astype(F32)
            key, value = head_pair(first[0:frames], second[0:frames], low)
            upper, lower = head_pair(first[frames:], second[frames:], low_part)
            cs = tile * LANES
            joined_ref[base : base + half, cs : cs + LANES] = upper.astype(BF16)
            joined_ref[base + half : base + frames, cs : cs + LANES] = lower.astype(BF16)
            joined_ref[base : base + frames, inner + cs : inner + cs + LANES] = key.astype(BF16)
            joined_ref[base : base + frames, 2 * inner + cs : 2 * inner + cs + LANES] = (
                value.astype(BF16)
            )
    order = one_hot_rows(rows, frames, records, True)
    joined = jnp.dot(order, joined_ref[...], preferred_element_type=F32).astype(BF16)
    upstream = lax.dot_general(joined, weight_ref[...], NT, preferred_element_type=F32)
    inputs = input_ref[...].reshape(rows, features).astype(F32)
    row_mean = jnp.mean(inputs, axis=-1, keepdims=True)
    centred = inputs - row_mean
    row_var = jnp.mean(centred * centred, axis=-1, keepdims=True)
    inv_std = lax.rsqrt(row_var + 1e-05)
    normed = centred * inv_std
    scaled = upstream * gain_ref[...].astype(F32)
    branch = inv_std * (
        scaled
        - jnp.mean(scaled, axis=-1, keepdims=True)
        - normed * jnp.mean(scaled * normed, axis=-1, keepdims=True)
    )
    total = grad_ref[...].reshape(rows, features).astype(F32) + branch
    out_ref[...] = total.astype(BF16).reshape(frames, records, features)


def per_device(
    layer_input,
    grad_out,
    queries,
    keys_saved,
    values_saved,
    out_weight,
    qkv_weight,
    ln_gain,
    lengths,
):
    frames, records, features = grad_out.shape[1:]
    inner = out_weight.shape[1]
    devices = lax.axis_size("seq")
    length = devices * frames
    packed = frames + frames // 2
    block = 256
    vmem = pltpu.CompilerParams(vmem_limit_bytes=48 * 1024 * 1024)

    sent = pl.pallas_call(
        pack_kernel,
        out_shape=jax.ShapeDtypeStruct((devices, frames, 2 * LANES), BF16),
        compiler_params=vmem,
        name="pack",
    )(grad_out[0], queries[0], keys_saved[0], values_saved[0], out_weight[0])
    heads = lax.all_to_all(sent, "seq", split_axis=0, concat_axis=0, tiled=True)
    whole = pl.BlockSpec(memory_space=pltpu.VMEM)
    back = pl.pallas_call(
        attend_kernel,
        out_shape=jax.ShapeDtypeStruct((devices, packed, LANES), BF16),
        in_specs=[pl.BlockSpec(memory_space=pltpu.SMEM), whole],
        out_specs=whole,
        scratch_shapes=[
            pltpu.VMEM((HD, length), BF16),
            pltpu.VMEM((length, LANES), BF16),
            pltpu.VMEM((length, LANES), BF16),
            pltpu.VMEM((length, LANES), F32),
            pltpu.VMEM((length, block), F32),
            pltpu.VMEM((length, block), F32),
            pltpu.VMEM((length, LANES), F32),
        ],
        compiler_params=vmem,
        name="attend",
    )(lengths, heads.reshape(length, 2 * LANES))
    back = lax.all_to_all(back, "seq", split_axis=0, concat_axis=0, tiled=True)
    total = pl.pallas_call(
        finish_kernel,
        out_shape=jax.ShapeDtypeStruct((frames, records, features), BF16),
        scratch_shapes=[pltpu.VMEM((frames * records, 3 * inner), BF16)],
        compiler_params=vmem,
        name="finish",
    )(back, qkv_weight[0], layer_input[0], grad_out[0], ln_gain)
    return passed_along(total, "pipe", -1)[None]


def solution(mesh):
    placed = (
        P("pipe", "seq", None, None),
        P("pipe", "seq", None, None),
        P("pipe", "seq", None, None),
        P("pipe", "seq", None, None),
        P("pipe", "seq", None, None),
        P("pipe", None, None),
        P("pipe", None, None),
        P("pipe", None),
        P("pipe", None),
    )
    return jax.shard_map(
        per_device,
        mesh=mesh,
        in_specs=placed,
        out_specs=P("pipe", "seq", None, None),
        check_vma=False,
    )
```

time: 234 us -> 118 us (0.50); the launches traced: 232 us -> 118 us
  blocking collectives: 0 us -> 78.5 us
  waiting for transfers between devices: 73.4 us -> 11.3 us
  local copies, waits for them, and re-layouts: 68.7 us -> 6.86 us
  starting transfers between devices: 46.1 us -> 3.26 us
  matrix products: 30 us -> 0 us
  Pallas kernels: 0 us -> 18.2 us
  other arithmetic: 11.1 us -> 0 us
    all_to_all x0 -> x2, blocking collectives: none -> 78.5 us  [the longest x1 48.2 us: per_device(): heads = lax.all_to_all(sent, 'seq', split_axis=0, concat_axis=0, tiled=True)]
    all_to_all x7 -> x0, waiting for transfers between devices: 60.5 us -> none  [the longest x1 12.5 us: per_device(): lax.all_to_all(query_cols, 'seq', split_axis=1, concat_axis=0, tiled=True)]
    all_to_all x7 -> x0, starting transfers between devices: 42.8 us -> none  [the longest x1 15.4 us: per_device(): lax.all_to_all(grad_cols, 'seq', split_axis=1, concat_axis=0, tiled=True)]
    dot_general x17 -> x0, matrix products: 30 us -> none  [the longest x3 10.8 us: one_block(): jnp.einsum('pqk,qph->kph', prob_low, grad_block, preferred_element_type=j...]
    pallas_call x0 -> x3, Pallas kernels: none -> 18.2 us  [the longest x1 10.3 us: per_device(): pl.pallas_call(attend_kernel, out_shape=jax.ShapeDtypeStruct((devices, pa...]
    unnamed x35 -> x19, local copies, waits for them, and re-layouts: 25 us -> 6.86 us
    all_to_all x16 -> x0, local copies, waits for them, and re-layouts: 17.5 us -> none  [the longest x4 7.62 us: per_device(): lax.all_to_all(grad_query, 'seq', split_axis=0, concat_axis=1, tiled=True)]
    reshape x8 -> x0, local copies, waits for them, and re-layouts: 12.3 us -> none  [the longest x1 2 us: per_device(): back_key.reshape(row_count, inner_width)]
  transfers between devices with their start and end apart: 8 -> 1, of which waited for: 7 -> 1; matrix products, arithmetic and copies ran while one was open for 18% -> 0% of each run, Pallas kernels for 0% -> 0%
where the time goes in v1:
time: 118 us
  blocking collectives  78.5 us (67%)
  Pallas kernels  18.2 us (15%)
  waiting for transfers between devices  11.3 us (10%)
  local copies, waits for them, and re-layouts  6.86 us (6%)
  starting transfers between devices  3.26 us (3%)
    all_to_all x1, blocking collectives, per_device(): heads = lax.all_to_all(sent, 'seq', split_axis=0, concat_axis=0, tiled=True)  48.2 us
    all_to_all x1, blocking collectives, per_device(): back = lax.all_to_all(back, 'seq', split_axis=0, concat_axis=0, tiled=True)  30.2 us
    ppermute x1, waiting for transfers between devices, passed_along(): return lax.ppermute(block, axis, route)  11.3 us
    pallas_call x1, Pallas kernels, per_device(): pl.pallas_call(attend_kernel, out_shape=jax.ShapeDtypeStruct((devices, pa...  10.3 us
    unnamed x19, local copies, waits for them, and re-layouts  6.86 us
    pallas_call x1, Pallas kernels, per_device(): pl.pallas_call(finish_kernel, out_shape=jax.ShapeDtypeStruct((frames, rec...  6.3 us
    ppermute x1, starting transfers between devices, passed_along(): return lax.ppermute(block, axis, route)  3.26 us
  transfers between devices with their start and end apart: 1, of which 1 were waited for; matrix products, arithmetic and copies ran while one was open for 0% of the time, Pallas kernels for 0%

profile of v1, /device:TPU:62, one launch (start us, length us, event | category | flops | bytes accessed | tf_op | source)
XLA Modules:
  0.0 118.1 jit_solution(6836953612525038873)
XLA Ops:
  0.0 0.0 copy-start.7
  0.0 0.0 copy-start
  0.0 1.7 %copy-done = bf16[1,768,1536]{2,1,0:T(8,128)(2,1)S(1)} copy-done((bf16[1,768,1536]{2,1,0:T(8,128)(2,1)S(1)}, bf16[1,768,1536]{2,1,0:T(8,128)(2,1)}, u32[]{:S(2)}) %copy-start) | copy-done | bytes 2359320
  1.7 0.0 copy-start.1
  1.7 1.0 copy-done.1
  2.7 0.0 copy-start.4
  2.7 0.9 copy-done.4
  3.6 0.0 copy-start.5
  3.6 0.9 copy-done.5
  4.5 0.0 copy-start.6
  4.5 0.9 copy-done.6
  5.5 0.0 copy-start.2
  5.5 0.0 copy-start.3
  5.5 1.6 %pack.1 = bf16[24,64,256]{2,1,0:T(8,128)(2,1)S(1)} custom-call(bf16[64,2,1536]{2,1,0:T(2,128)(2,1)S(1)} %bitcast.11, bf16[64,2,768]{2,1,0:T(2,128)(2,1)S(1)} %bitcast.14, bf16[64,2,768]{2,1,0:T(2,128)(2,1)S(1)} %bitcast.15, bf16[64,2,768]{2,1,0:T(2,128)(2,1)S(1)} %bitcast.16, bf16[768,1536]{1,0:T(8,128)(2,1)S(1)} %bitcast.10), custom_call_target="tpu_custom_call" | custom-call | tf_op jit(solution)/shard_map/pack/pallas_call | solution.py:212
  7.1 48.2 %all_to_all.10 = bf16[24,64,256]{2,1,0:T(8,128)(2,1)S(1)} all-to-all(bf16[24,64,256]{2,1,0:T(8,128)(2,1)S(1)} %pack.1), channel_id=1, replica_groups=mesh['pipe'=32,'seq'=24] {'seq'}, dimensions={0} | all-to-all | bytes 1572864 | tf_op jit(solution)/shard_map/all_to_all | solution.py:218
  55.3 0.0 copy-start.8
  55.3 0.7 copy-done.8
  56.0 10.3 %attend.1 = bf16[24,96,128]{2,1,0:T(8,128)(2,1)S(1)} custom-call(s32[1,2]{1,0:T(1,128)S(1)} %copy-done.8, bf16[1536,256]{1,0:T(8,128)(2,1)S(1)} %bitcast.9), custom_call_target="tpu_custom_call" | custom-call | tf_op jit(solution)/shard_map/attend/pallas_call | solution.py:220
  66.2 30.2 %all_to_all.11.back_ref = bf16[24,96,128]{2,1,0:T(8,128)(2,1)S(1)} all-to-all(bf16[24,96,128]{2,1,0:T(8,128)(2,1)S(1)} %attend.1), channel_id=1, replica_groups=mesh['pipe'=32,'seq'=24] {'seq'}, dimensions={0} | all-to-all | bytes 1179648 | tf_op jit(solution)/shard_map/all_to_all | solution.py:237
  96.5 0.0 copy-done.7
  96.5 0.0 copy-done.2
  96.5 0.0 copy-done.3
  96.5 6.3 %finish.1 = bf16[64,2,1536]{2,1,0:T(2,128)(2,1)S(1)} custom-call(bf16[24,96,128]{2,1,0:T(8,128)(2,1)S(1)} %all_to_all.11.back_ref, bf16[1536,2304]{1,0:T(8,128)(2,1)} %bitcast.17, bf16[64,2,1536]{2,1,0:T(2,128)(2,1)S(1)} %bitcast.13, bf16[64,2,1536]{2,1,0:T(2,128)(2,1)S(1)} %bitcast.12, bf16[1,1536]{1,0:T(2,128)(2,1)S(1)} %copy-done.7), custom_call_target="tpu_custom_call" | custom-call | tf_op jit(solution)/shard_map/finish/pallas_call | solution.py:238
  102.8 3.3 %collective-permute-start = (bf16[64,2,1536]{2,1,0:T(2,128)(2,1)S(1)}, bf16[64,2,1536]{2,1,0:T(2,128)(2,1)S(1)}, u32[]{:S(2)}, u32[]{:S(2)}) collective-permute-start(bf16[64,2,1536]{2,1,0:T(2,128)(2,1)S(1)} %finish.1), channel_id=1, source_target_pairs={{24,0},{48,24},{72,48},{96,72},{120,96},{144,120},{168,144},{192,1... | collective-permute-start | bytes 1179656 | tf_op jit(solution)/shard_map/ppermute | solution.py:21
  106.1 11.3 %collective-permute-done = bf16[64,2,1536]{2,1,0:T(2,128)(2,1)S(1)} collective-permute-done((bf16[64,2,1536]{2,1,0:T(2,128)(2,1)S(1)}, bf16[64,2,1536]{2,1,0:T(2,128)(2,1)S(1)}, u32[]{:S(2)}, u32[]{:S(2)}) %collective-permute-start) | collective-permute-done | bytes 393248 | tf_op jit(solution)/shard_map/ppermute | solution.py:21
  117.3 0.7 copy.11
Async XLA Ops:
  0.0 96.5 %copy-start.7 = (bf16[1,1536]{1,0:T(2,128)(2,1)S(1)}, bf16[1,1536]{1,0:T(2,128)(2,1)}, u32[]{:S(2)}) copy-start(bf16[1,1536]{1,0:T(2,128)(2,1)} %gain_ref.1) | copy-start | bytes 9220
  0.0 1.7 %copy-start = (bf16[1,768,1536]{2,1,0:T(8,128)(2,1)S(1)}, bf16[1,768,1536]{2,1,0:T(8,128)(2,1)}, u32[]{:S(2)}) copy-start(bf16[1,768,1536]{2,1,0:T(8,128)(2,1)} %param.14) | copy-start | bytes 7077892
  1.7 1.0 copy-start.1
  2.7 0.9 copy-start.4
  3.6 0.9 copy-start.5
  4.5 0.9 copy-start.6
  5.5 91.0 %copy-start.2 = (bf16[1,64,2,1536]{3,2,1,0:T(2,128)(2,1)S(1)}, bf16[1,64,2,1536]{3,2,1,0:T(2,128)(2,1)}, u32[]{:S(2)}) copy-start(bf16[1,64,2,1536]{3,2,1,0:T(2,128)(2,1)} %param.10) | copy-start | bytes 1179652
  5.5 91.0 %copy-start.3 = (bf16[1,64,2,1536]{3,2,1,0:T(2,128)(2,1)S(1)}, bf16[1,64,2,1536]{3,2,1,0:T(2,128)(2,1)}, u32[]{:S(2)}) copy-start(bf16[1,64,2,1536]{3,2,1,0:T(2,128)(2,1)} %param.9) | copy-start | bytes 1179652
  55.3 0.7 copy-start.8
  102.8 14.5 %collective-permute-start = (bf16[64,2,1536]{2,1,0:T(2,128)(2,1)S(1)}, bf16[64,2,1536]{2,1,0:T(2,128)(2,1)S(1)}, u32[]{:S(2)}, u32[]{:S(2)}) collective-permute-start(bf16[64,2,1536]{2,1,0:T(2,128)(2,1)S(1)} %finish.1), channel_id=1, source_target_pairs={{24,0},{48,24},{72,48},{96,72},{120,96},{144,120},{168,144},{192,1... | collective-permute-start | bytes 1179656 | tf_op jit(solution)/shard_map/ppermute | solution.py:21

commit v2 on v1

--- a/solution.py
+++ b/solution.py
@@ -39,46 +39,90 @@
     return jnp.where(low, left, turned), jnp.where(low, turned, right)
 
 
-def pack_kernel(grad_ref, query_ref, key_ref, value_ref, weight_ref, sent_ref):
+def pack_kernel(
+    grad_hbm,
+    query_hbm,
+    key_hbm,
+    value_hbm,
+    weight_hbm,
+    sent_ref,
+    grad_ref,
+    query_ref,
+    key_ref,
+    value_ref,
+    weight_ref,
+    sems,
+):
     frames, records, features = grad_ref.shape
     inner = weight_ref.shape[0]
     rows = frames * records
+    loads = [
+        pltpu.make_async_copy(source, target, sems.at[n])
+        for n, (source, target) in enumerate(
+            (
+                (key_hbm, key_ref),
+                (value_hbm, value_ref),
+                (grad_hbm, grad_ref),
+                (query_hbm, query_ref),
+                (weight_hbm, weight_ref),
+            )
+        )
+    ]
+    for load in loads:
+        load.start()
     order = one_hot_rows(rows, frames, records, False)
 
     def by_record(matrix):
         return jnp.dot(order, matrix, preferred_element_type=F32)
 
+    low = low_half((frames, LANES))
+
+    def place(first, second, start):
+        for record in range(records):
+            rs = slice(record * frames, (record + 1) * frames)
+            for tile in range(inner // LANES):
+                cs = slice(tile * LANES, (tile + 1) * LANES)
+                pair = record * HEADS_W + 2 * tile
+                sides = head_pair(first[rs, cs], second[rs, cs], low)
+                for side in range(2):
+                    sent_ref[pair + side, :, start : start + LANES] = sides[side].astype(BF16)
+
+    loads[0].wait()
+    loads[1].wait()
+    key = by_record(key_ref[...].reshape(rows, inner))
+    value = by_record(value_ref[...].reshape(rows, inner))
+    place(key, value, LANES)
+    for load in loads[2:]:
+        load.wait()
+    query = by_record(query_ref[...].reshape(rows, inner))
     flat_grad = grad_ref[...].reshape(rows, features)
     heads_grad = lax.dot_general(
         flat_grad, weight_ref[...], NT, preferred_element_type=F32
     ).astype(BF16)
-    grad = by_record(heads_grad)
-    query = by_record(query_ref[...].reshape(rows, inner))
-    key = by_record(key_ref[...].reshape(rows, inner))
-    value = by_record(value_ref[...].reshape(rows, inner))
-    low = low_half((frames, LANES))
-    for record in range(records):
-        rs = slice(record * frames, (record + 1) * frames)
-        for tile in range(inner // LANES):
-            cs = slice(tile * LANES, (tile + 1) * LANES)
-            pair = record * HEADS_W + 2 * tile
-            qg = head_pair(query[rs, cs], grad[rs, cs], low)
-            kv = head_pair(key[rs, cs], value[rs, cs], low)
-            for side in range(2):
-                sent_ref[pair + side, :, 0:LANES] = qg[side].astype(BF16)
-                sent_ref[pair + side, :, LANES:] = kv[side].astype(BF16)
+    place(query, by_record(heads_grad), 0)
 
 
 def attend_kernel(
-    length_ref, heads_ref, back_ref, kt_ref, q_ref, g_ref, bias_ref, score_ref, prob_ref, acc_ref
+    length_hbm,
+    heads_ref,
+    back_ref,
+    kt_ref,
+    q_ref,
+    g_ref,
+    bias_ref,
+    score_ref,
+    prob_ref,
+    acc_ref,
+    length_ref,
+    sem,
 ):
+    load = pltpu.make_async_copy(length_hbm, length_ref, sem)
+    load.start()
     length = heads_ref.shape[0]
     devices, packed, _ = back_ref.shape
     frames = length // devices
     block = 256
     chunks = length // block
-    record = lax.axis_index("seq") // HEADS_W
-    key_length = jnp.where(record == 0, length_ref[0, 0], length_ref[0, 1])
     factor = HD ** (-0.5)
     rate = factor * LOG2E
 
@@ -87,6 +131,9 @@
     q_ref[...] = jnp.where(low, both, 0.0).astype(BF16)
     g_ref[...] = jnp.where(low, 0.0, both).astype(BF16)
     kt_ref[...] = heads_ref[:, LANES:].astype(F32).T[0:HD].astype(BF16)
+    load.wait()
+    record = lax.axis_index("seq") // HEADS_W
+    key_length = jnp.where(record == 0, length_ref[0, 0], length_ref[0, 1])
     bias_ref[...] = jnp.where(
         lax.broadcasted_iota(jnp.int32, (length, LANES), 0) < key_length, 0.0, MASKED
     )
@@ -207,20 +254,36 @@
     length = devices * frames
     packed = frames + frames // 2
     block = 256
-    vmem = pltpu.CompilerParams(vmem_limit_bytes=48 * 1024 * 1024)
+    vmem = pltpu.CompilerParams(vmem_limit_bytes=24 * 1024 * 1024)
+    far = pl.BlockSpec(memory_space=pltpu.HBM)
+    whole = pl.BlockSpec(memory_space=pltpu.VMEM)
 
     sent = pl.pallas_call(
         pack_kernel,
         out_shape=jax.ShapeDtypeStruct((devices, frames, 2 * LANES), BF16),
+        in_specs=[far] * 5,
+        out_specs=whole,
+        scratch_shapes=[
+            pltpu.VMEM((frames, records, features), BF16),
+            pltpu.VMEM((frames, records, inner), BF16),
+            pltpu.VMEM((frames, records, inner), BF16),
+            pltpu.VMEM((frames, records, inner), BF16),
+            pltpu.VMEM((inner, features), BF16),
+            pltpu.SemaphoreType.DMA((5,)),
+        ],
         compiler_params=vmem,
         name="pack",
-    )(grad_out[0], queries[0], keys_saved[0], values_saved[0], out_weight[0])
+    )(
+        *(
+            pltpu.with_memory_space_constraint(array[0], pltpu.HBM)
+            for array in (grad_out, queries, keys_saved, values_saved, out_weight)
+        )
+    )
     heads = lax.all_to_all(sent, "seq", split_axis=0, concat_axis=0, tiled=True)
-    whole = pl.BlockSpec(memory_space=pltpu.VMEM)
     back = pl.pallas_call(
         attend_kernel,
         out_shape=jax.ShapeDtypeStruct((devices, packed, LANES), BF16),
-        in_specs=[pl.BlockSpec(memory_space=pltpu.SMEM), whole],
+        in_specs=[far, whole],
         out_specs=whole,
         scratch_shapes=[
             pltpu.VMEM((HD, length), BF16),
@@ -230,10 +293,12 @@
             pltpu.VMEM((length, block), F32),
             pltpu.VMEM((length, block), F32),
             pltpu.VMEM((length, LANES), F32),
+            pltpu.SMEM(lengths.shape, jnp.int32),
+            pltpu.SemaphoreType.DMA,
         ],
         compiler_params=vmem,
         name="attend",
-    )(lengths, heads.reshape(length, 2 * LANES))
+    )(pltpu.with_memory_space_constraint(lengths, pltpu.HBM), heads.reshape(length, 2 * LANES))
     back = lax.all_to_all(back, "seq", split_axis=0, concat_axis=0, tiled=True)
     total = pl.pallas_call(
         finish_kernel,

time: 118 us -> 111 us (0.941)
  local copies, waits for them, and re-layouts: 6.86 us -> 0.76 us
  Pallas kernels: 18.2 us -> 16.9 us
    unnamed x19 -> x9, local copies, waits for them, and re-layouts: 6.86 us -> 0.76 us
    pallas_call x1, Pallas kernels: 6.3 us -> 3.34 us  [per_device(): pl.pallas_call(finish_kernel, out_shape=jax.ShapeDtypeStruct((frames, rec...]
    pallas_call x1, Pallas kernels: 1.6 us -> 3.32 us  [per_device(): pl.pallas_call(pack_kernel, out_shape=jax.ShapeDtypeStruct((devices, fram...]
where the time goes in v2:
time: 111 us
  blocking collectives  78.5 us (71%)
  Pallas kernels  16.9 us (15%)
  waiting for transfers between devices  11.3 us (10%)
  starting transfers between devices  3.26 us (3%)
    all_to_all x1, blocking collectives, per_device(): heads = lax.all_to_all(sent, 'seq', split_axis=0, concat_axis=0, tiled=True)  48.2 us
    all_to_all x1, blocking collectives, per_device(): back = lax.all_to_all(back, 'seq', split_axis=0, concat_axis=0, tiled=True)  30.2 us
    ppermute x1, waiting for transfers between devices, passed_along(): return lax.ppermute(block, axis, route)  11.3 us
    pallas_call x1, Pallas kernels, per_device(): pl.pallas_call(attend_kernel, out_shape=jax.ShapeDtypeStruct((devices, pa...  10.2 us
    pallas_call x1, Pallas kernels, per_device(): pl.pallas_call(finish_kernel, out_shape=jax.ShapeDtypeStruct((frames, rec...  3.34 us
    pallas_call x1, Pallas kernels, per_device(): pl.pallas_call(pack_kernel, out_shape=jax.ShapeDtypeStruct((devices, fram...  3.32 us
    ppermute x1, starting transfers between devices, passed_along(): return lax.ppermute(block, axis, route)  3.26 us
  transfers between devices with their start and end apart: 1, of which 1 were waited for; matrix products, arithmetic and copies ran while one was open for 0% of the time, Pallas kernels for 0%

profile of v2, /device:TPU:62, one launch (start us, length us, event | category | flops | bytes accessed | tf_op | source)
XLA Modules:
  0.0 110.7 jit_solution(937394040447251990)
XLA Ops:
  0.0 0.0 copy-start.1
  0.0 0.0 copy-start.3
  0.0 0.0 copy-start
  0.0 0.0 copy-start.2
  0.0 3.3 %pack.1 = bf16[24,64,256]{2,1,0:T(8,128)(2,1)S(1)} custom-call(bf16[64,2,1536]{2,1,0:T(2,128)(2,1)} %bitcast.11, bf16[64,2,768]{2,1,0:T(2,128)(2,1)} %bitcast.16, bf16[64,2,768]{2,1,0:T(2,128)(2,1)} %bitcast.17, bf16[64,2,768]{2,1,0:T(2,128)(2,1)} %bitcast.18, bf16[768,1536]{1,0:T(8,128)(2,1)} %bitcast.14), custom_call_target="tpu_custom_call" | custom-call | tf_op jit(solution)/shard_map/pack/pallas_call | solution.py:261
  3.4 48.2 %all_to_all.10 = bf16[24,64,256]{2,1,0:T(8,128)(2,1)S(1)} all-to-all(bf16[24,64,256]{2,1,0:T(8,128)(2,1)S(1)} %pack.1), channel_id=1, replica_groups=mesh['pipe'=32,'seq'=24] {'seq'}, dimensions={0} | all-to-all | bytes 1572864 | tf_op jit(solution)/shard_map/all_to_all | solution.py:282
  51.6 10.2 %attend.1 = bf16[24,96,128]{2,1,0:T(8,128)(2,1)S(1)} custom-call(s32[1,2]{1,0:T(1,128)} %length_hbm.1, bf16[1536,256]{1,0:T(8,128)(2,1)S(1)} %bitcast.10), custom_call_target="tpu_custom_call" | custom-call | tf_op jit(solution)/shard_map/attend/pallas_call | solution.py:283
  61.8 30.2 %all_to_all.11.back_ref = bf16[24,96,128]{2,1,0:T(8,128)(2,1)S(1)} all-to-all(bf16[24,96,128]{2,1,0:T(8,128)(2,1)S(1)} %attend.1), channel_id=1, replica_groups=mesh['pipe'=32,'seq'=24] {'seq'}, dimensions={0} | all-to-all | bytes 1179648 | tf_op jit(solution)/shard_map/all_to_all | solution.py:302
  92.0 0.0 copy-done.1
  92.0 0.0 copy-done.3
  92.0 0.0 copy-done
  92.0 0.0 copy-done.2
  92.1 3.3 %finish.1 = bf16[64,2,1536]{2,1,0:T(2,128)(2,1)S(1)} custom-call(bf16[24,96,128]{2,1,0:T(8,128)(2,1)S(1)} %all_to_all.11.back_ref, bf16[1536,2304]{1,0:T(8,128)(2,1)S(1)} %bitcast.9, bf16[64,2,1536]{2,1,0:T(2,128)(2,1)S(1)} %bitcast.13, bf16[64,2,1536]{2,1,0:T(2,128)(2,1)S(1)} %bitcast.12, bf16[1,1536]{1,0:T(2,128)(2,1)S(1)} %copy-done.3), custom_call_target="tpu_custom_call" | custom-call | tf_op jit(solution)/shard_map/finish/pallas_call | solution.py:303
  95.4 3.3 %collective-permute-start = (bf16[64,2,1536]{2,1,0:T(2,128)(2,1)S(1)}, bf16[64,2,1536]{2,1,0:T(2,128)(2,1)S(1)}, u32[]{:S(2)}, u32[]{:S(2)}) collective-permute-start(bf16[64,2,1536]{2,1,0:T(2,128)(2,1)S(1)} %finish.1), channel_id=1, source_target_pairs={{24,0},{48,24},{72,48},{96,72},{120,96},{144,120},{168,144},{192,1... | collective-permute-start | bytes 1179656 | tf_op jit(solution)/shard_map/ppermute | solution.py:21
  98.7 11.3 %collective-permute-done = bf16[64,2,1536]{2,1,0:T(2,128)(2,1)S(1)} collective-permute-done((bf16[64,2,1536]{2,1,0:T(2,128)(2,1)S(1)}, bf16[64,2,1536]{2,1,0:T(2,128)(2,1)S(1)}, u32[]{:S(2)}, u32[]{:S(2)}) %collective-permute-start) | collective-permute-done | bytes 393248 | tf_op jit(solution)/shard_map/ppermute | solution.py:21
  110.0 0.7 copy.11
Async XLA Ops:
  0.0 92.0 %copy-start.1 = (bf16[1,64,2,1536]{3,2,1,0:T(2,128)(2,1)S(1)}, bf16[1,64,2,1536]{3,2,1,0:T(2,128)(2,1)}, u32[]{:S(2)}) copy-start(bf16[1,64,2,1536]{3,2,1,0:T(2,128)(2,1)} %param.10) | copy-start | bytes 1179652
  0.0 92.0 %copy-start.3 = (bf16[1,1536]{1,0:T(2,128)(2,1)S(1)}, bf16[1,1536]{1,0:T(2,128)(2,1)}, u32[]{:S(2)}) copy-start(bf16[1,1536]{1,0:T(2,128)(2,1)} %gain_ref.1) | copy-start | bytes 9220
  0.0 92.0 %copy-start = (bf16[1,1536,2304]{2,1,0:T(8,128)(2,1)S(1)}, bf16[1,1536,2304]{2,1,0:T(8,128)(2,1)}, u32[]{:S(2)}) copy-start(bf16[1,1536,2304]{2,1,0:T(8,128)(2,1)} %param.15) | copy-start | bytes 21233668
  0.0 92.0 %copy-start.2 = (bf16[1,64,2,1536]{3,2,1,0:T(2,128)(2,1)S(1)}, bf16[1,64,2,1536]{3,2,1,0:T(2,128)(2,1)}, u32[]{:S(2)}) copy-start(bf16[1,64,2,1536]{3,2,1,0:T(2,128)(2,1)} %param.9) | copy-start | bytes 1179652
  95.4 14.5 %collective-permute-start = (bf16[64,2,1536]{2,1,0:T(2,128)(2,1)S(1)}, bf16[64,2,1536]{2,1,0:T(2,128)(2,1)S(1)}, u32[]{:S(2)}, u32[]{:S(2)}) collective-permute-start(bf16[64,2,1536]{2,1,0:T(2,128)(2,1)S(1)} %finish.1), channel_id=1, source_target_pairs={{24,0},{48,24},{72,48},{96,72},{120,96},{144,120},{168,144},{192,1... | collective-permute-start | bytes 1179656 | tf_op jit(solution)/shard_map/ppermute | solution.py:21

commit v3 on v2

--- a/solution.py
+++ b/solution.py
@@ -107,10 +107,9 @@
     heads_ref,
     back_ref,
     kt_ref,
-    q_ref,
-    g_ref,
+    gq_ref,
     bias_ref,
-    score_ref,
+    terms_ref,
     prob_ref,
     acc_ref,
     length_ref,
@@ -121,15 +120,19 @@
     length = heads_ref.shape[0]
     devices, packed, _ = back_ref.shape
     frames = length // devices
-    block = 256
-    chunks = length // block
+    block = terms_ref.shape[2]
+    chunk = 128
     factor = HD ** (-0.5)
     rate = factor * LOG2E
 
     low = low_half((length, LANES))
     both = heads_ref[:, 0:LANES].astype(F32)
-    q_ref[...] = jnp.where(low, both, 0.0).astype(BF16)
-    g_ref[...] = jnp.where(low, 0.0, both).astype(BF16)
+    only_g = jnp.where(low, 0.0, both).astype(BF16)
+    only_q = jnp.where(low, both, 0.0).astype(BF16)
+    for qb in range(length // block):
+        rows = slice(qb * block, (qb + 1) * block)
+        gq_ref[2 * qb * block : (2 * qb + 1) * block, :] = only_g[rows]
+        gq_ref[(2 * qb + 1) * block : (2 * qb + 2) * block, :] = only_q[rows]
     kt_ref[...] = heads_ref[:, LANES:].astype(F32).T[0:HD].astype(BF16)
     load.wait()
     record = lax.axis_index("seq") // HEADS_W
@@ -141,57 +144,74 @@
     def fold(values, op):
         return op(values.reshape(-1, 8, block), axis=0)
 
-    for qb in range(chunks):
-        qs = slice(qb * block, (qb + 1) * block)
-        q_blk = q_ref[qs, :]
-        g_blk = g_ref[qs, :]
-        peak = None
-        for c in range(chunks):
-            ks = slice(c * block, (c + 1) * block)
-            bias = bias_ref[ks, :]
-            scores = lax.dot_general(
-                heads_ref[ks, LANES:], q_blk, NT, preferred_element_type=F32
-            ) + jnp.concatenate([bias] * (block // LANES), axis=1)
-            score_ref[ks, :] = scores
-            part = fold(scores, jnp.max)
-            peak = part if peak is None else jnp.maximum(peak, part)
-        peak = jnp.max(peak, axis=0, keepdims=True)
-        total = None
-        weighted = None
-        for c in range(chunks):
-            ks = slice(c * block, (c + 1) * block)
-            terms = jnp.exp2((score_ref[ks, :] - peak) * rate)
-            grad_prob = lax.dot_general(
-                heads_ref[ks, LANES:], g_blk, NT, preferred_element_type=F32
-            )
-            score_ref[ks, :] = terms
-            prob_ref[ks, :] = grad_prob
-            part = fold(terms, jnp.sum)
-            total = part if total is None else total + part
-            part = fold(terms * grad_prob, jnp.sum)
-            weighted = part if weighted is None else weighted + part
+    def first_stage(qb, c, state):
+        ks = slice(c * chunk, (c + 1) * chunk)
+        g_blk = gq_ref[2 * qb * block : (2 * qb + 1) * block, :]
+        q_blk = gq_ref[(2 * qb + 1) * block : (2 * qb + 2) * block, :]
+        bias = jnp.concatenate([bias_ref[ks, :]] * (block // LANES), axis=1)
+        scores = (
+            lax.dot_general(heads_ref[ks, LANES:], q_blk, NT, preferred_element_type=F32) + bias
+        )
+        peak = jnp.max(fold(scores, jnp.max), axis=0, keepdims=True)
+        terms = jnp.exp2((scores - peak) * rate)
+        grad_prob = lax.dot_general(
+            heads_ref[ks, LANES:], g_blk, NT, preferred_element_type=F32
+        )
+        terms_ref[qb % 2, ks, :] = terms
+        prob_ref[qb % 2, ks, :] = grad_prob
+        state["peaks"].append(peak)
+        state["sums"].append(fold(terms, jnp.sum))
+        state["weighted"].append(fold(terms * grad_prob, jnp.sum))
+
+    def row_totals(state):
+        top = state["peaks"][0]
+        for peak in state["peaks"][1:]:
+            top = jnp.maximum(top, peak)
+        scales = [jnp.exp2((peak - top) * rate) for peak in state["peaks"]]
+        total = sum(part * scale for part, scale in zip(state["sums"], scales))
+        weighted = sum(part * scale for part, scale in zip(state["weighted"], scales))
         share = 1.0 / jnp.sum(total, axis=0, keepdims=True)
-        delta = jnp.sum(weighted, axis=0, keepdims=True) * share
-        grad_q = None
-        for c in range(chunks):
-            ks = slice(c * block, (c + 1) * block)
-            prob = score_ref[ks, :] * share
-            grad_score = (prob * (prob_ref[ks, :] - delta)).astype(BF16)
-            update = jnp.dot(prob.astype(BF16), g_blk, preferred_element_type=F32) + jnp.dot(
-                grad_score, q_blk, preferred_element_type=F32
-            )
-            if qb == 0:
-                acc_ref[ks, :] = update
-            else:
-                acc_ref[ks, :] += update
-            part = jnp.dot(kt_ref[:, ks], grad_score, preferred_element_type=F32)
-            grad_q = part if grad_q is None else grad_q + part
-        rows = (grad_q.T * factor).reshape(block // frames, frames, HD)
+        state["delta"] = jnp.sum(weighted, axis=0, keepdims=True) * share
+        state["shares"] = [share * scale for scale in scales]
+        state["grad_q"] = 0.0
+
+    def last_stage(qb, c, state):
+        ks = slice(c * chunk, (c + 1) * chunk)
+        prob = terms_ref[qb % 2, ks, :] * state["shares"][c]
+        grad_score = (prob * (prob_ref[qb % 2, ks, :] - state["delta"])).astype(BF16)
+        update = jnp.dot(
+            jnp.concatenate([prob.astype(BF16), grad_score], axis=1),
+            gq_ref[2 * qb * block : (2 * qb + 2) * block, :],
+            preferred_element_type=F32,
+        )
+        if qb == 0:
+            acc_ref[ks, :] = update
+        else:
+            acc_ref[ks, :] += update
+        state["grad_q"] = state["grad_q"] + jnp.dot(
+            kt_ref[:, ks], grad_score, preferred_element_type=F32
+        )
+
+    def send_queries(qb, state):
+        rows = (state["grad_q"].T * factor).reshape(block // frames, frames, HD)
         half = frames // 2
         for j in range(block // frames):
             back_ref[qb * (block // frames) + j, frames:packed, :] = jnp.concatenate(
                 [rows[j, 0:half], rows[j, half:]], axis=1
             ).astype(BF16)
+
+    blocks = length // block
+    states = [dict(peaks=[], sums=[], weighted=[]) for _ in range(blocks)]
+    for qb in range(blocks + 1):
+        for c in range(length // chunk):
+            if qb < blocks:
+                first_stage(qb, c, states[qb])
+            if qb > 0:
+                last_stage(qb - 1, c, states[qb - 1])
+        if qb < blocks:
+            row_totals(states[qb])
+        if qb > 0:
+            send_queries(qb - 1, states[qb - 1])
     scale = jnp.where(low_half((1, LANES)), factor, 1.0)
     back_ref[:, 0:frames, :] = (acc_ref[...] * scale).astype(BF16).reshape(devices, frames, LANES)
 
@@ -271,7 +291,7 @@
             pltpu.VMEM((inner, features), BF16),
             pltpu.SemaphoreType.DMA((5,)),
         ],
-        compiler_params=vmem,
+        compiler_params=pltpu.CompilerParams(vmem_limit_bytes=50 * 1024 * 1024),
         name="pack",
     )(
         *(
@@ -287,16 +307,20 @@
         out_specs=whole,
         scratch_shapes=[
             pltpu.VMEM((HD, length), BF16),
-            pltpu.VMEM((length, LANES), BF16),
-            pltpu.VMEM((length, LANES), BF16),
+            pltpu.VMEM((2 * length, LANES), BF16),
             pltpu.VMEM((length, LANES), F32),
-            pltpu.VMEM((length, block), F32),
-            pltpu.VMEM((length, block), F32),
+            pltpu.VMEM((2, length, block), F32),
+            pltpu.VMEM((2, length, block), F32),
             pltpu.VMEM((length, LANES), F32),
             pltpu.SMEM(lengths.shape, jnp.int32),
             pltpu.SemaphoreType.DMA,
         ],
         compiler_params=vmem,
+        cost_estimate=pl.CostEstimate(
+            flops=64 * length * length * HD,
+            bytes_accessed=8 * length * LANES,
+            transcendentals=length * length,
+        ),
         name="attend",
     )(pltpu.with_memory_space_constraint(lengths, pltpu.HBM), heads.reshape(length, 2 * LANES))
     back = lax.all_to_all(back, "seq", split_axis=0, concat_axis=0, tiled=True)

time: 111 us -> 109 us (0.982)
  Pallas kernels: 16.9 us -> 15.1 us
    pallas_call x1, Pallas kernels: 10.2 us -> 8.51 us  [per_device(): pl.pallas_call(attend_kernel, out_shape=jax.ShapeDtypeStruct((devices, pa...]
where the time goes in v3:
time: 109 us
  blocking collectives  78.7 us (72%)
  Pallas kernels  15.1 us (14%)
  waiting for transfers between devices  11.3 us (10%)
  starting transfers between devices  3.24 us (3%)
    all_to_all x1, blocking collectives, per_device(): heads = lax.all_to_all(sent, 'seq', split_axis=0, concat_axis=0, tiled=True)  48.5 us
    all_to_all x1, blocking collectives, per_device(): back = lax.all_to_all(back, 'seq', split_axis=0, concat_axis=0, tiled=True)  30.2 us
    ppermute x1, waiting for transfers between devices, passed_along(): return lax.ppermute(block, axis, route)  11.3 us
    pallas_call x1, Pallas kernels, per_device(): pl.pallas_call(attend_kernel, out_shape=jax.ShapeDtypeStruct((devices, pa...  8.51 us
    pallas_call x1, Pallas kernels, per_device(): pl.pallas_call(finish_kernel, out_shape=jax.ShapeDtypeStruct((frames, rec...  3.35 us
    ppermute x1, starting transfers between devices, passed_along(): return lax.ppermute(block, axis, route)  3.24 us
    pallas_call x1, Pallas kernels, per_device(): pl.pallas_call(pack_kernel, out_shape=jax.ShapeDtypeStruct((devices, fram...  3.2 us
  transfers between devices with their start and end apart: 1, of which 1 were waited for; matrix products, arithmetic and copies ran while one was open for 0% of the time, Pallas kernels for 0%

profile of v3, /device:TPU:62, one launch (start us, length us, event | category | flops | bytes accessed | tf_op | source)
XLA Modules:
  0.0 109.2 jit_solution(17361026475787998547)
XLA Ops:
  0.0 3.2 %pack.1 = bf16[24,64,256]{2,1,0:T(8,128)(2,1)S(1)} custom-call(bf16[64,2,1536]{2,1,0:T(2,128)(2,1)} %bitcast.12, bf16[64,2,768]{2,1,0:T(2,128)(2,1)} %bitcast.18, bf16[64,2,768]{2,1,0:T(2,128)(2,1)} %bitcast.19, bf16[64,2,768]{2,1,0:T(2,128)(2,1)} %bitcast.20, bf16[768,1536]{1,0:T(8,128)(2,1)} %bitcast.16), custom_call_target="tpu_custom_call" | custom-call | tf_op jit(solution)/shard_map/pack/pallas_call | solution.py:281
  3.2 0.0 slice-start
  3.2 48.5 %all_to_all.10 = bf16[24,64,256]{2,1,0:T(8,128)(2,1)S(1)} all-to-all(bf16[24,64,256]{2,1,0:T(8,128)(2,1)S(1)} %pack.1), channel_id=1, replica_groups=mesh['pipe'=32,'seq'=24] {'seq'}, dimensions={0} | all-to-all | bytes 1572864 | tf_op jit(solution)/shard_map/all_to_all | solution.py:302
  51.7 0.0 slice-start.1
  51.7 0.0 copy-start
  51.7 0.0 copy-start.1
  51.7 0.0 copy-start.2
  51.7 8.5 %attend.1 = bf16[24,96,128]{2,1,0:T(8,128)(2,1)S(1)} custom-call(s32[1,2]{1,0:T(1,128)} %length_hbm.1, bf16[1536,256]{1,0:T(8,128)(2,1)S(1)} %bitcast.14), custom_call_target="tpu_custom_call" | custom-call | flops 9663676416 | bytes 1572864 | tf_op jit(solution)/shard_map/attend/pallas_call | solution.py:303
  60.3 30.2 %all_to_all.11.back_ref = bf16[24,96,128]{2,1,0:T(8,128)(2,1)S(1)} all-to-all(bf16[24,96,128]{2,1,0:T(8,128)(2,1)S(1)} %attend.1), channel_id=1, replica_groups=mesh['pipe'=32,'seq'=24] {'seq'}, dimensions={0} | all-to-all | bytes 1179648 | tf_op jit(solution)/shard_map/all_to_all | solution.py:326
  90.5 0.0 slice-done
  90.5 0.0 slice-done.1
  90.5 0.0 copy-done
  90.5 0.0 copy-done.1
  90.5 0.0 copy-done.2
  90.5 3.3 %finish.1 = bf16[64,2,1536]{2,1,0:T(2,128)(2,1)S(1)} custom-call(bf16[24,96,128]{2,1,0:T(8,128)(2,1)S(1)} %all_to_all.11.back_ref, bf16[1536,2304]{1,0:T(8,128)(2,1)S(1)} %bitcast.11, bf16[64,2,1536]{2,1,0:T(2,128)(2,1)S(1)} %bitcast.15, bf16[64,2,1536]{2,1,0:T(2,128)(2,1)S(1)} %bitcast.13, bf16[1,1536]{1,0:T(2,128)(2,1)S(1)} %copy-done.2), custom_call_target="tpu_custom_call" | custom-call | tf_op jit(solution)/shard_map/finish/pallas_call | solution.py:327
  93.9 3.2 %collective-permute-start = (bf16[64,2,1536]{2,1,0:T(2,128)(2,1)S(1)}, bf16[64,2,1536]{2,1,0:T(2,128)(2,1)S(1)}, u32[]{:S(2)}, u32[]{:S(2)}) collective-permute-start(bf16[64,2,1536]{2,1,0:T(2,128)(2,1)S(1)} %finish.1), channel_id=1, source_target_pairs={{24,0},{48,24},{72,48},{96,72},{120,96},{144,120},{168,144},{192,1... | collective-permute-start | bytes 1179656 | tf_op jit(solution)/shard_map/ppermute | solution.py:21
  97.1 11.3 %collective-permute-done = bf16[64,2,1536]{2,1,0:T(2,128)(2,1)S(1)} collective-permute-done((bf16[64,2,1536]{2,1,0:T(2,128)(2,1)S(1)}, bf16[64,2,1536]{2,1,0:T(2,128)(2,1)S(1)}, u32[]{:S(2)}, u32[]{:S(2)}) %collective-permute-start) | collective-permute-done | bytes 393248 | tf_op jit(solution)/shard_map/ppermute | solution.py:21
  108.4 0.7 copy.11
  (1 shorter events, 0.0 us)
Async XLA Ops:
  3.2 87.3 %slice-start = ((s8[7077888]{0:T(1024)(128)(4,1)}), s8[4194304]{0:T(1024)(128)(4,1)S(1)}, s32[]{:S(2)}) async-start(s8[7077888]{0:T(1024)(128)(4,1)} %bitcast.9), calls=%async_computation.2 | async-start | bytes 8388608
  51.7 38.8 %slice-start.1 = ((s8[7077888]{0:T(1024)(128)(4,1)}), s8[2883584]{0:T(1024)(128)(4,1)S(1)}, s32[]{:S(2)}) async-start(s8[7077888]{0:T(1024)(128)(4,1)} %bitcast.9), calls=%async_computation.3 | async-start | bytes 5767168
  51.7 38.8 %copy-start = (bf16[1,64,2,1536]{3,2,1,0:T(2,128)(2,1)S(1)}, bf16[1,64,2,1536]{3,2,1,0:T(2,128)(2,1)}, u32[]{:S(2)}) copy-start(bf16[1,64,2,1536]{3,2,1,0:T(2,128)(2,1)} %param.10) | copy-start | bytes 1179652
  51.7 38.8 %copy-start.1 = (bf16[1,64,2,1536]{3,2,1,0:T(2,128)(2,1)S(1)}, bf16[1,64,2,1536]{3,2,1,0:T(2,128)(2,1)}, u32[]{:S(2)}) copy-start(bf16[1,64,2,1536]{3,2,1,0:T(2,128)(2,1)} %param.9) | copy-start | bytes 1179652
  51.7 38.8 %copy-start.2 = (bf16[1,1536]{1,0:T(2,128)(2,1)S(1)}, bf16[1,1536]{1,0:T(2,128)(2,1)}, u32[]{:S(2)}) copy-start(bf16[1,1536]{1,0:T(2,128)(2,1)} %gain_ref.1) | copy-start | bytes 9220
  93.9 14.5 %collective-permute-start = (bf16[64,2,1536]{2,1,0:T(2,128)(2,1)S(1)}, bf16[64,2,1536]{2,1,0:T(2,128)(2,1)S(1)}, u32[]{:S(2)}, u32[]{:S(2)}) collective-permute-start(bf16[64,2,1536]{2,1,0:T(2,128)(2,1)S(1)} %finish.1), channel_id=1, source_target_pairs={{24,0},{48,24},{72,48},{96,72},{120,96},{144,120},{168,144},{192,1... | collective-permute-start | bytes 1179656 | tf_op jit(solution)/shard_map/ppermute | solution.py:21

commit v4 on v3

--- a/solution.py
+++ b/solution.py
@@ -92,14 +92,15 @@
     key = by_record(key_ref[...].reshape(rows, inner))
     value = by_record(value_ref[...].reshape(rows, inner))
     place(key, value, LANES)
-    for load in loads[2:]:
-        load.wait()
+    loads[2].wait()
+    flat_grad = by_record(grad_ref[...].reshape(rows, features)).astype(BF16)
+    loads[3].wait()
     query = by_record(query_ref[...].reshape(rows, inner))
-    flat_grad = grad_ref[...].reshape(rows, features)
+    loads[4].wait()
     heads_grad = lax.dot_general(
         flat_grad, weight_ref[...], NT, preferred_element_type=F32
-    ).astype(BF16)
-    place(query, by_record(heads_grad), 0)
+    )
+    place(query, heads_grad.astype(BF16).astype(F32), 0)
 
 
 def attend_kernel(
@@ -291,7 +292,7 @@
             pltpu.VMEM((inner, features), BF16),
             pltpu.SemaphoreType.DMA((5,)),
         ],
-        compiler_params=pltpu.CompilerParams(vmem_limit_bytes=50 * 1024 * 1024),
+        compiler_params=vmem,
         name="pack",
     )(
         *(
@@ -316,11 +317,6 @@
             pltpu.SemaphoreType.DMA,
         ],
         compiler_params=vmem,
-        cost_estimate=pl.CostEstimate(
-            flops=64 * length * length * HD,
-            bytes_accessed=8 * length * LANES,
-            transcendentals=length * length,
-        ),
         name="attend",
     )(pltpu.with_memory_space_constraint(lengths, pltpu.HBM), heads.reshape(length, 2 * LANES))
     back = lax.all_to_all(back, "seq", split_axis=0, concat_axis=0, tiled=True)

time: 109 us -> 109 us (level)
  no operation moved by 1% of the time
where the time goes in v4:
time: 109 us
  blocking collectives  78.6 us (72%)
  Pallas kernels  15 us (14%)
  waiting for transfers between devices  11.3 us (10%)
  starting transfers between devices  3.26 us (3%)
    all_to_all x1, blocking collectives, per_device(): heads = lax.all_to_all(sent, 'seq', split_axis=0, concat_axis=0, tiled=True)  48.4 us
    all_to_all x1, blocking collectives, per_device(): back = lax.all_to_all(back, 'seq', split_axis=0, concat_axis=0, tiled=True)  30.2 us
    ppermute x1, waiting for transfers between devices, passed_along(): return lax.ppermute(block, axis, route)  11.3 us
    pallas_call x1, Pallas kernels, per_device(): pl.pallas_call(attend_kernel, out_shape=jax.ShapeDtypeStruct((devices, pa...  8.37 us
    pallas_call x1, Pallas kernels, per_device(): pl.pallas_call(finish_kernel, out_shape=jax.ShapeDtypeStruct((frames, rec...  3.33 us
    ppermute x1, starting transfers between devices, passed_along(): return lax.ppermute(block, axis, route)  3.26 us
    pallas_call x1, Pallas kernels, per_device(): pl.pallas_call(pack_kernel, out_shape=jax.ShapeDtypeStruct((devices, fram...  3.26 us
  transfers between devices with their start and end apart: 1, of which 1 were waited for; matrix products, arithmetic and copies ran while one was open for 0% of the time, Pallas kernels for 0%

profile of v4, /device:TPU:62, one launch (start us, length us, event | category | flops | bytes accessed | tf_op | source)
XLA Modules:
  0.0 108.9 jit_solution(18048920514606008264)
XLA Ops:
  0.0 0.0 copy-start.1
  0.0 0.0 copy-start.3
  0.0 0.0 copy-start
  0.0 0.0 copy-start.2
  0.0 3.3 %pack.1 = bf16[24,64,256]{2,1,0:T(8,128)(2,1)S(1)} custom-call(bf16[64,2,1536]{2,1,0:T(2,128)(2,1)} %bitcast.11, bf16[64,2,768]{2,1,0:T(2,128)(2,1)} %bitcast.16, bf16[64,2,768]{2,1,0:T(2,128)(2,1)} %bitcast.17, bf16[64,2,768]{2,1,0:T(2,128)(2,1)} %bitcast.18, bf16[768,1536]{1,0:T(8,128)(2,1)} %bitcast.14), custom_call_target="tpu_custom_call" | custom-call | tf_op jit(solution)/shard_map/pack/pallas_call | solution.py:282
  3.3 48.4 %all_to_all.10 = bf16[24,64,256]{2,1,0:T(8,128)(2,1)S(1)} all-to-all(bf16[24,64,256]{2,1,0:T(8,128)(2,1)S(1)} %pack.1), channel_id=1, replica_groups=mesh['pipe'=32,'seq'=24] {'seq'}, dimensions={0} | all-to-all | bytes 1572864 | tf_op jit(solution)/shard_map/all_to_all | solution.py:303
  51.7 8.4 %attend.1 = bf16[24,96,128]{2,1,0:T(8,128)(2,1)S(1)} custom-call(s32[1,2]{1,0:T(1,128)} %length_hbm.1, bf16[1536,256]{1,0:T(8,128)(2,1)S(1)} %bitcast.10), custom_call_target="tpu_custom_call" | custom-call | tf_op jit(solution)/shard_map/attend/pallas_call | solution.py:304
  60.0 30.2 %all_to_all.11.back_ref = bf16[24,96,128]{2,1,0:T(8,128)(2,1)S(1)} all-to-all(bf16[24,96,128]{2,1,0:T(8,128)(2,1)S(1)} %attend.1), channel_id=1, replica_groups=mesh['pipe'=32,'seq'=24] {'seq'}, dimensions={0} | all-to-all | bytes 1179648 | tf_op jit(solution)/shard_map/all_to_all | solution.py:322
  90.3 0.0 copy-done.1
  90.3 0.0 copy-done.3
  90.3 0.0 copy-done
  90.3 0.0 copy-done.2
  90.3 3.3 %finish.1 = bf16[64,2,1536]{2,1,0:T(2,128)(2,1)S(1)} custom-call(bf16[24,96,128]{2,1,0:T(8,128)(2,1)S(1)} %all_to_all.11.back_ref, bf16[1536,2304]{1,0:T(8,128)(2,1)S(1)} %bitcast.9, bf16[64,2,1536]{2,1,0:T(2,128)(2,1)S(1)} %bitcast.13, bf16[64,2,1536]{2,1,0:T(2,128)(2,1)S(1)} %bitcast.12, bf16[1,1536]{1,0:T(2,128)(2,1)S(1)} %copy-done.3), custom_call_target="tpu_custom_call" | custom-call | tf_op jit(solution)/shard_map/finish/pallas_call | solution.py:323
  93.6 3.3 %collective-permute-start = (bf16[64,2,1536]{2,1,0:T(2,128)(2,1)S(1)}, bf16[64,2,1536]{2,1,0:T(2,128)(2,1)S(1)}, u32[]{:S(2)}, u32[]{:S(2)}) collective-permute-start(bf16[64,2,1536]{2,1,0:T(2,128)(2,1)S(1)} %finish.1), channel_id=1, source_target_pairs={{24,0},{48,24},{72,48},{96,72},{120,96},{144,120},{168,144},{192,1... | collective-permute-start | bytes 1179656 | tf_op jit(solution)/shard_map/ppermute | solution.py:21
  96.9 11.3 %collective-permute-done = bf16[64,2,1536]{2,1,0:T(2,128)(2,1)S(1)} collective-permute-done((bf16[64,2,1536]{2,1,0:T(2,128)(2,1)S(1)}, bf16[64,2,1536]{2,1,0:T(2,128)(2,1)S(1)}, u32[]{:S(2)}, u32[]{:S(2)}) %collective-permute-start) | collective-permute-done | bytes 393248 | tf_op jit(solution)/shard_map/ppermute | solution.py:21
  108.2 0.7 copy.11
Async XLA Ops:
  0.0 90.3 %copy-start.1 = (bf16[1,64,2,1536]{3,2,1,0:T(2,128)(2,1)S(1)}, bf16[1,64,2,1536]{3,2,1,0:T(2,128)(2,1)}, u32[]{:S(2)}) copy-start(bf16[1,64,2,1536]{3,2,1,0:T(2,128)(2,1)} %param.10) | copy-start | bytes 1179652
  0.0 90.3 %copy-start.3 = (bf16[1,1536]{1,0:T(2,128)(2,1)S(1)}, bf16[1,1536]{1,0:T(2,128)(2,1)}, u32[]{:S(2)}) copy-start(bf16[1,1536]{1,0:T(2,128)(2,1)} %gain_ref.1) | copy-start | bytes 9220
  0.0 90.3 %copy-start = (bf16[1,1536,2304]{2,1,0:T(8,128)(2,1)S(1)}, bf16[1,1536,2304]{2,1,0:T(8,128)(2,1)}, u32[]{:S(2)}) copy-start(bf16[1,1536,2304]{2,1,0:T(8,128)(2,1)} %param.15) | copy-start | bytes 21233668
  0.0 90.3 %copy-start.2 = (bf16[1,64,2,1536]{3,2,1,0:T(2,128)(2,1)S(1)}, bf16[1,64,2,1536]{3,2,1,0:T(2,128)(2,1)}, u32[]{:S(2)}) copy-start(bf16[1,64,2,1536]{3,2,1,0:T(2,128)(2,1)} %param.9) | copy-start | bytes 1179652
  93.6 14.6 %collective-permute-start = (bf16[64,2,1536]{2,1,0:T(2,128)(2,1)S(1)}, bf16[64,2,1536]{2,1,0:T(2,128)(2,1)S(1)}, u32[]{:S(2)}, u32[]{:S(2)}) collective-permute-start(bf16[64,2,1536]{2,1,0:T(2,128)(2,1)S(1)} %finish.1), channel_id=1, source_target_pairs={{24,0},{48,24},{72,48},{96,72},{120,96},{144,120},{168,144},{192,1... | collective-permute-start | bytes 1179656 | tf_op jit(solution)/shard_map/ppermute | solution.py:21
